TPU v7x, 32 devices: a whole 2x2x4 slice. The times are simulated.
32 devices in a mesh: dp: 4 (over y, x), tm: 2 (over core), space: 4 (over z).
Axes of the slice: x: 2, y: 2, z: 4, core: 2. Of those that a mesh axis runs over, the one named last changes fastest.
Arguments:
- video: bfloat16 [4, 8, 64, 128, 128], P('dp', 'tm', 'space'), may hold values from -6 to 6
- lengths: int32 [4], P('dp'), may hold values from 2 to 8
- norm_gain: float32 [128], replicated, may hold values from 0.25 to 1.75
- norm_shift: float32 [128], replicated, may hold values from -3 to 3
- kernel: bfloat16 [3, 3, 3, 128, 128], replicated, may hold values from -0.109375 to 0.109375
- conv_bias: float32 [128], replicated, may hold values from -3 to 3
- cotangent: bfloat16 [4, 8, 64, 128, 128], P('dp', 'tm', 'space'), may hold values from -0.01171875 to 0.01171875
Outputs:
- output: bfloat16 [4, 8, 64, 128, 128], P('dp', 'tm', 'space')
- grad_kernel: float32 [3, 3, 3, 128, 128], replicated
- grad_bias: float32 [128], replicated
All inputs are finite; a program needn't handle non-finite values.
Results may differ from a plain program's by a relative error of at most 0.0032.
Values may be sent and summed in bfloat16 or wider, within the bound.
No kernel may reach another device: no remote copies, remote signals or barrier semaphores. Data moves between devices by JAX's collectives and lax.ppermute only.
A program may use at most 128 MiB of HBM per device.

v0:
```python
import jax
import jax.numpy as jnp
from jax import lax
from jax.sharding import PartitionSpec as P

GROUPS = 32


def shifted(array, axis, by):
    length = lax.axis_size(axis)
    pairs = [(i, i + by) for i in range(length) if 0 <= i + by < length]
    return lax.ppermute(array, axis, pairs)


def padded_2(block, sides, width):
    for axis, dim in sides:
        count = lax.axis_size(axis)
        forward = [(i, i + 1) for i in range(count - 1)]
        backward = [(target, source) for source, target in forward]
        low = lax.ppermute(
            lax.slice_in_dim(block, block.shape[dim] - width, None, axis=dim), axis, forward
        )
        high = lax.ppermute(lax.slice_in_dim(block, 0, width, axis=dim), axis, backward)
        block = jnp.concatenate([low, block, high], axis=dim)
    return block


def body(video, lengths, norm_gain, norm_shift, kernel, conv_bias, cotangent):
    frames = video.shape[1]
    rows = video.shape[2]
    cols = video.shape[3]
    chans = video.shape[4]
    per = chans // GROUPS
    first = lax.axis_index("tm") * frames
    valid = (first + jnp.arange(frames, dtype=jnp.int32) < lengths[0]).astype(jnp.float32)
    mask = valid[:, None, None, None]
    grouped = video[0].reshape(frames, rows, cols, GROUPS, per)
    gmask = valid[:, None, None, None, None]
    count = lengths[0].astype(jnp.float32) * (rows * lax.axis_size("space")) * cols * per
    local_sum = jnp.sum(grouped * gmask, axis=(0, 1, 2, 4), dtype=jnp.float32)
    mean = lax.psum(local_sum, ("tm", "space")) / count
    spread = (grouped.astype(jnp.float32) - mean[:, None]) * gmask
    variance = lax.psum(jnp.sum(spread * spread, axis=(0, 1, 2, 4)), ("tm", "space")) / count
    normed = (grouped.astype(jnp.float32) - mean[:, None]) * lax.rsqrt(variance + 1e-05)[:, None]
    normed = normed.reshape(frames, rows, cols, chans) * norm_gain + norm_shift
    activated = (jax.nn.silu(normed) * mask).astype(jnp.bfloat16)[None]
    earlier = shifted(activated[:, frames - 2 :], "tm", 1)
    timed = jnp.concatenate([earlier, activated], axis=1)
    extended = padded_2(timed, (("space", 2),), 1)
    padded = jnp.pad(extended[0], ((0, 0), (0, 0), (1, 1), (0, 0)))
    masked = (cotangent[0].astype(jnp.float32) * mask).astype(jnp.bfloat16)
    stacked = jnp.concatenate(
        [
            jnp.pad(masked, ((0, 0), (0, 0), (shift_cols, 2 - shift_cols), (0, 0)))
            for shift_cols in range(3)
        ],
        axis=-1,
    )
    stacked = stacked.reshape(-1, 3 * chans)
    wide_rows = frames * rows * (cols + 2)
    partial_value = jnp.zeros((wide_rows, 3 * chans), jnp.float32)
    grads = []
    for kt in range(3):
        for ky in range(3):
            band = padded[kt : kt + frames, ky : ky + rows].reshape(wide_rows, chans)
            taps = jnp.transpose(kernel[kt, ky], (1, 0, 2)).reshape(chans, 3 * chans)
            partial_value = partial_value + jnp.dot(band, taps, preferred_element_type=jnp.float32)
            product = lax.dot_general(
                band, stacked, (((0,), (0,)), ((), ())), preferred_element_type=jnp.float32
            )
            grads.append(
                jnp.transpose(product.reshape(chans, 3, chans), (1, 0, 2)).reshape(3 * chans, chans)
            )
    partial_value = partial_value.reshape(frames, rows, cols + 2, 3 * chans)
    conv = (
        partial_value[:, :, 0:cols, 0:chans]
        + partial_value[:, :, 1 : cols + 1, chans : 2 * chans]
        + partial_value[:, :, 2 : cols + 2, 2 * chans : 3 * chans]
    )
    output = ((video[0].astype(jnp.float32) + conv + conv_bias) * mask).astype(jnp.bfloat16)[None]
    local_kernel = jnp.concatenate(grads, axis=0)
    local_bias = jnp.sum(masked.reshape(-1, chans).astype(jnp.float32), axis=0)
    summed, grad_bias = lax.psum((local_kernel, local_bias), ("dp", "tm", "space"))
    return (output, summed.reshape(3, 3, 3, chans, chans), grad_bias)


def solution(mesh):
    return jax.shard_map(
        body,
        mesh=mesh,
        in_specs=(
            P("dp", "tm", "space", None, None),
            P("dp"),
            P(),
            P(),
            P(),
            P(),
            P("dp", "tm", "space", None, None),
        ),
        out_specs=(P("dp", "tm", "space", None, None), P(), P()),
        check_vma=False,
    )
```

profile of v0, /device:TPU:0, one launch (start us, length us, event | category | flops | bytes accessed | tf_op | source)
XLA Modules:
  0.0 367.3 jit_solution(12672691524185307099)
XLA Ops:
  8.0 2.8 fusion.26
  10.8 0.1 reduce_sum.32
  11.0 0.1 reduce_sum.36
  11.1 18.5 %psum.28 = f32[32]{0:T(128)S(1)} all-reduce(f32[32]{0:T(128)S(1)} %reduce_sum.36), channel_id=1, replica_groups=mesh['dp'=4,'tm'=2,'space'=4] {'tm','space'}, use_global_device_ids=true, to_apply=%region_2.0 | all-reduce | flops 32 | bytes 256 | tf_op jit(solution)/shard_map/psum | solution.py:41
  29.7 0.1 sub.20
  29.8 3.3 convert_reduce_fusion
  33.2 0.1 reduce_sum.46
  33.3 13.7 %psum.29 = f32[32]{0:T(128)S(1)} all-reduce(f32[32]{0:T(128)S(1)} %reduce_sum.46), channel_id=1, replica_groups=mesh['dp'=4,'tm'=2,'space'=4] {'tm','space'}, use_global_device_ids=true, to_apply=%region_5.6 | all-reduce | flops 32 | bytes 256 | tf_op jit(solution)/shard_map/psum | solution.py:43
  47.1 0.1 mul.88
  47.2 1.6 fusion.18
  49.0 2.6 collective-permute-start
  51.6 2.2 collective-permute-done
  53.8 0.8 pad_maximum_fusion.1
  54.6 3.9 %collective-permute-start.1 = (bf16[1,6,1,128,128]{4,3,2,1,0:T(8,128)(2,1)}, bf16[1,6,1,128,128]{4,3,2,1,0:T(8,128)(2,1)}, u32[]{:S(2)}, u32[]{:S(2)}) collective-permute-start(bf16[1,6,1,128,128]{4,3,2,1,0:T(8,128)(2,1)} %get-tuple-element.14), channel_id=1, source_target_pairs={{0,1},{1,2},{2,3},{4,5},{5,6},{6,7},{8,9},{9,10},{10,11},{12,13},{... | collective-permute-start | bytes 589832 | tf_op jit(solution)/shard_map/ppermute | solution.py:20
  58.5 1.7 collective-permute-start.2
  60.3 0.8 fusion.46
  61.2 1.6 copy.65
  62.8 1.6 copy.64
  64.4 1.6 copy.63
  66.0 1.6 copy.62
  67.7 1.6 copy.61
  69.3 1.6 copy.60
  70.9 0.7 copy.59
  71.7 0.1 copy.58
  71.8 0.1 copy.57
  72.0 2.0 maximum_bitcast_fusion
  74.0 10.9 %pad_slice_fusion = (bf16[4,16,130,128]{3,2,1,0:T(8,128)(2,1)}, bf16[4,16,130,128]{3,2,1,0:T(8,128)(2,1)}, bf16[4,16,130,128]{3,2,1,0:T(8,128)(2,1)}, bf16[4,16,...) fusion(bf16[6,18,128,128]{3,2,1,0:T(8,128)(2,1)S(1)} %maximum_b, ...), kind=kLoop, calls=%fused_computation.67 | loop fusion | bytes 22708224 | tf_op jit(solution)/shard_map/slice | solution.py:65
  84.9 4.1 %reshape.166 = bf16[8320,128]{1,0:T(8,128)(2,1)} reshape(bf16[4,16,130,128]{3,2,1,0:T(8,128)(2,1)} %get-tuple-element.5) | data formatting | bytes 4259840 | tf_op jit(solution)/shard_map/reshape | solution.py:65
  89.0 4.0 %reshape.152 = bf16[8320,128]{1,0:T(8,128)(2,1)} reshape(bf16[4,16,130,128]{3,2,1,0:T(8,128)(2,1)} %get-tuple-element.6) | data formatting | bytes 4259840 | tf_op jit(solution)/shard_map/reshape | solution.py:65
  93.0 4.0 %reshape.154 = bf16[8320,128]{1,0:T(8,128)(2,1)} reshape(bf16[4,16,130,128]{3,2,1,0:T(8,128)(2,1)} %get-tuple-element.7) | data formatting | bytes 4259840 | tf_op jit(solution)/shard_map/reshape | solution.py:65
  97.0 4.0 %reshape.156 = bf16[8320,128]{1,0:T(8,128)(2,1)} reshape(bf16[4,16,130,128]{3,2,1,0:T(8,128)(2,1)} %get-tuple-element.8) | data formatting | bytes 4259840 | tf_op jit(solution)/shard_map/reshape | solution.py:65
  101.1 4.0 %reshape.158 = bf16[8320,128]{1,0:T(8,128)(2,1)} reshape(bf16[4,16,130,128]{3,2,1,0:T(8,128)(2,1)} %get-tuple-element.9) | data formatting | bytes 4259840 | tf_op jit(solution)/shard_map/reshape | solution.py:65
  105.1 4.1 %reshape.160 = bf16[8320,128]{1,0:T(8,128)(2,1)} reshape(bf16[4,16,130,128]{3,2,1,0:T(8,128)(2,1)} %get-tuple-element.10) | data formatting | bytes 4259840 | tf_op jit(solution)/shard_map/reshape | solution.py:65
  109.2 4.0 %reshape.162 = bf16[8320,128]{1,0:T(8,128)(2,1)} reshape(bf16[4,16,130,128]{3,2,1,0:T(8,128)(2,1)} %get-tuple-element.11) | data formatting | bytes 4259840 | tf_op jit(solution)/shard_map/reshape | solution.py:65
  113.3 4.0 %reshape.164 = bf16[8320,128]{1,0:T(8,128)(2,1)} reshape(bf16[4,16,130,128]{3,2,1,0:T(8,128)(2,1)} %get-tuple-element.12) | data formatting | bytes 4259840 | tf_op jit(solution)/shard_map/reshape | solution.py:65
  117.3 4.1 %reshape.150 = bf16[8320,128]{1,0:T(8,128)(2,1)} reshape(bf16[4,16,130,128]{3,2,1,0:T(8,128)(2,1)} %get-tuple-element.13) | data formatting | bytes 4259840 | tf_op jit(solution)/shard_map/reshape | solution.py:65
  121.4 3.4 fusion.47
  124.9 3.6 convolution_add_fusion.7
  128.5 3.6 convolution_add_fusion.6
  132.1 3.6 convolution_add_fusion.5
  135.7 3.6 convolution_add_fusion.4
  139.3 3.6 convolution_add_fusion.3
  143.0 3.6 convolution_add_fusion.2
  146.6 3.8 %convolution_add_fusion.1 = f32[8320,384]{1,0:T(8,128)S(1)} fusion(f32[8320,384]{1,0:T(8,128)S(1)} %convolution_add_fusion.2, bf16[8320,128]{1,0:T(8,128)(2,1)} %reshape.164, bf16[128,384]{0,1:T(8,128)(2,1)S(1)} %bitcast.176), kind=kOutput, calls=%fused_computation.3 | convolution fusion | flops 821084160 | bytes 27787264 | tf_op jit(solution)/shard_map/dot_general | solution.py:67
  150.4 8.2 %convolution_add_fusion = f32[8320,384]{1,0:T(8,128)} fusion(f32[8320,384]{1,0:T(8,128)S(1)} %convolution_add_fusion.1, bf16[8320,128]{1,0:T(8,128)(2,1)} %reshape.166, bf16[128,384]{0,1:T(8,128)(2,1)S(1)} %bitcast.175), kind=kOutput, calls=%fused_computation.2 | convolution fusion | flops 821084160 | bytes 27787264 | tf_op jit(solution)/shard_map/dot_general | solution.py:67
  158.6 12.0 %reshape.168 = f32[4,16,130,384]{3,2,1,0:T(8,128)} reshape(f32[8320,384]{1,0:T(8,128)} %convolution_add_fusion) | data formatting | bytes 25559040 | tf_op jit(solution)/shard_map/reshape | solution.py:74
  170.6 7.8 %fusion.20 = (bf16[4,16,128,128]{3,2,1,0:T(8,128)(2,1)S(1)}, bf16[1,4,16,128,128]{4,3,2,1,0:T(8,128)(2,1)}) fusion(bf16[1,4,16,128,128]{4,3,2,1,0:T(8,128)(2,1)} %param.13, f32[4]{0:T(128)S(1)} %compare_convert_fusion, f32[128]{0:T(128)S(1)} %copy-done.23, f32[4,16,130,384]{3,2,1,0:T(8,128)} %reshape.168, bf16[1,4,16,128,128]{4,3,2,1,0:T(8,128)(2,1)S(1)} %copy-done.1), kind=kLoop, calls=%fused_computation.37 | loop fusion | flops 10485760 | bytes 20972048 | tf_op jit(solution)/shard_map/convert_element_type | solution.py:51
  178.4 3.9 %fusion.5 = bf16[4,16,130,384]{3,2,1,0:T(8,128)(2,1)} fusion(bf16[4,16,128,128]{3,2,1,0:T(8,128)(2,1)S(1)} %get-tuple-element.25), kind=kLoop, calls=%fused_computation.17 | loop fusion | flops 44728320 | bytes 8486912 | tf_op jit(solution)/shard_map/concatenate | solution.py:52
  182.4 8.5 %reshape.169 = bf16[8320,384]{1,0:T(8,128)(2,1)} reshape(bf16[4,16,130,384]{3,2,1,0:T(8,128)(2,1)} %fusion.5) | data formatting | bytes 12779520 | tf_op jit(solution)/shard_map/reshape | solution.py:59
  190.9 9.4 %copy.29 = bf16[384,8320]{1,0:T(8,128)(2,1)} copy(bf16[384,8320]{0,1:T(8,128)(2,1)} %bitcast.163) | data formatting | bytes 12779520 | tf_op jit(solution)/shard_map/dot_general | solution.py:68
  200.3 4.9 %fusion.27 = f32[128,3,128]{2,0,1:T(8,128)S(1)} fusion(bf16[3,128,8320]{2,1,0:T(8,128)(2,1)} %bitcast.154, bf16[8320,128]{1,0:T(8,128)(2,1)S(1)} %copy-done.5), kind=kOutput, calls=%fused_computation.48 | convolution fusion | flops 817889280 | bytes 8716288 | tf_op jit(solution)/shard_map/dot_general | solution.py:68
  205.3 0.3 copy-done.9
  205.6 2.0 fusion.29
  207.6 2.0 fusion.31
  209.6 2.0 fusion.33
  211.6 2.0 fusion.35
  213.6 2.0 fusion.37
  215.7 2.0 fusion.39
  217.7 2.0 fusion.41
  219.7 2.0 fusion.43
  221.9 1.2 copy-done.12
  223.1 41.4 %psum.31 = f32[128]{0:T(128)} all-reduce(f32[128]{0:T(128)S(1)} %copy-done.24), channel_id=1, replica_groups=mesh['dp'=4,'tm'=2,'space'=4] {'dp','tm','space'}, use_global_device_ids=true, to_apply=%region_8.9 | all-reduce | flops 128 | bytes 1024 | tf_op jit(solution)/shard_map/psum | solution.py:83
  264.5 92.7 %all-reduce.6.cloned.1.call-done = f32[3,3,3,128,128]{4,3,2,1,0:T(8,128)} async-done(((f32[3,3,3,128,128]{4,3,2,1,0:T(8,128)}), f32[3,3,3,128,128]{4,3,2,1,0:T(8,128)}) %all-reduce.6.cloned.1.call-update) | async-done | bytes 1769488 | tf_op jit(solution)/shard_map/psum | solution.py:83
  357.2 2.9 copy.76
  (68 shorter events, 0.6 us)
Async XLA Ops:
  7.2 22.6 %copy-start.1 = (bf16[1,4,16,128,128]{4,3,2,1,0:T(8,128)(2,1)S(1)}, bf16[1,4,16,128,128]{4,3,2,1,0:T(8,128)(2,1)}, u32[]{:S(2)}) copy-start(bf16[1,4,16,128,128]{4,3,2,1,0:T(8,128)(2,1)} %param.7) | copy-start | bytes 6291460
  7.2 40.0 %copy-start.21 = (f32[128]{0:T(128)S(1)}, f32[128]{0:T(128)}, u32[]{:S(2)}) copy-start(f32[128]{0:T(128)} %param.10) | copy-start | bytes 1540
  7.2 40.0 %copy-start.22 = (f32[128]{0:T(128)S(1)}, f32[128]{0:T(128)}, u32[]{:S(2)}) copy-start(f32[128]{0:T(128)} %param.9) | copy-start | bytes 1540
  7.2 350.0 %all-reduce.6.cloned.1.call-start = ((), (), s32[]{:S(2)}) async-start(), calls=%async_computation | async-start | bytes 3538944 | tf_op jit(solution)/shard_map/psum | solution.py:83
  48.9 12.3 %copy-start.10 = (bf16[1,4,16,128,128]{4,3,2,1,0:T(8,128)(2,1)}, bf16[1,4,16,128,128]{4,3,2,1,0:T(8,128)(2,1)S(1)}, u32[]{:S(2)}) copy-start(bf16[1,4,16,128,128]{4,3,2,1,0:T(8,128)(2,1)S(1)} %fusion.18) | copy-start | bytes 6291460
  48.9 11.4 %copy-start.13 = (bf16[3,3,3,128,128]{4,3,2,1,0:T(8,128)(2,1)S(1)}, bf16[3,3,3,128,128]{4,3,2,1,0:T(8,128)(2,1)}, u32[]{:S(2)}) copy-start(bf16[3,3,3,128,128]{4,3,2,1,0:T(8,128)(2,1)} %param.11) | copy-start | bytes 2654212
  49.0 4.8 %collective-permute-start = (bf16[1,2,16,128,128]{4,3,2,1,0:T(8,128)(2,1)S(1)}, bf16[1,2,16,128,128]{4,3,2,1,0:T(8,128)(2,1)S(1)}, u32[]{:S(2)}, u32[]{:S(2)}) collective-permute-start(bf16[1,2,16,128,128]{4,3,2,1,0:T(8,128)(2,1)S(1)} %slice.96), channel_id=1, source_target_pairs={{0,4},{1,5},{2,6},{3,7},{8,12},{9,13},{10,14},{11,15},{16,20},{17,... | collective-permute-start | bytes 3145736 | tf_op jit(solution)/shard_map/ppermute | solution.py:12
  54.6 17.3 %collective-permute-start.1 = (bf16[1,6,1,128,128]{4,3,2,1,0:T(8,128)(2,1)}, bf16[1,6,1,128,128]{4,3,2,1,0:T(8,128)(2,1)}, u32[]{:S(2)}, u32[]{:S(2)}) collective-permute-start(bf16[1,6,1,128,128]{4,3,2,1,0:T(8,128)(2,1)} %get-tuple-element.14), channel_id=1, source_target_pairs={{0,1},{1,2},{2,3},{4,5},{5,6},{6,7},{8,9},{9,10},{10,11},{12,13},{... | collective-permute-start | bytes 589832 | tf_op jit(solution)/shard_map/ppermute | solution.py:20
  58.5 13.4 %collective-permute-start.2 = (bf16[1,6,1,128,128]{4,3,2,1,0:T(8,128)(2,1)}, bf16[1,6,1,128,128]{4,3,2,1,0:T(8,128)(2,1)}, u32[]{:S(2)}, u32[]{:S(2)}) collective-permute-start(bf16[1,6,1,128,128]{4,3,2,1,0:T(8,128)(2,1)} %get-tuple-element.15), channel_id=1, source_target_pairs={{1,0},{2,1},{3,2},{5,4},{6,5},{7,6},{9,8},{10,9},{11,10},{13,12},{... | collective-permute-start | bytes 589832 | tf_op jit(solution)/shard_map/ppermute | solution.py:23
  124.9 3.6 copy-start.20
  128.5 3.6 copy-start.19
  132.1 3.6 copy-start.18
  135.7 3.6 copy-start.17
  139.3 3.6 copy-start.16
  143.0 3.6 copy-start.15
  146.6 3.8 %copy-start.14 = (bf16[1,1,3,128,128]{3,4,2,1,0:T(8,128)(2,1)S(1)}, bf16[1,1,3,128,128]{3,4,2,1,0:T(8,128)(2,1)}, u32[]{:S(2)}) copy-start(bf16[1,1,3,128,128]{3,4,2,1,0:T(8,128)(2,1)} %copy.65) | copy-start | bytes 294916
  158.6 12.0 %copy-start.23 = (f32[128]{0:T(128)S(1)}, f32[128]{0:T(128)}, u32[]{:S(2)}) copy-start(f32[128]{0:T(128)} %param.12) | copy-start | bytes 1540
  190.9 9.4 %copy-start.5 = (bf16[8320,128]{1,0:T(8,128)(2,1)S(1)}, bf16[8320,128]{1,0:T(8,128)(2,1)}, u32[]{:S(2)}) copy-start(bf16[8320,128]{1,0:T(8,128)(2,1)} %reshape.166) | copy-start | bytes 6389764
  200.3 5.0 %copy-start = (bf16[384,8320]{1,0:T(8,128)(2,1)S(1)}, bf16[384,8320]{1,0:T(8,128)(2,1)}, u32[]{:S(2)}) copy-start(bf16[384,8320]{1,0:T(8,128)(2,1)} %copy.29) | copy-start | bytes 19169284
  200.3 5.3 %copy-start.9 = (bf16[8320,128]{1,0:T(8,128)(2,1)S(1)}, bf16[8320,128]{1,0:T(8,128)(2,1)}, u32[]{:S(2)}) copy-start(bf16[8320,128]{1,0:T(8,128)(2,1)} %reshape.164) | copy-start | bytes 6389764
  205.6 2.0 copy-start.8
  207.6 2.0 copy-start.7
  209.6 2.0 copy-start.6
  211.6 2.0 copy-start.4
  213.6 2.0 copy-start.3
  215.6 2.0 copy-start.2
  217.7 2.0 copy-start.11
  221.7 1.5 copy-start.24
  221.9 1.2 copy-start.12
Sparse Core Ops, SparseCore 0:
  223.2 133.9 all-reduce.5
where the time goes:
time: 373 us; the launch traced here: 367 us
  waiting for transfers between devices  94.9 us (25%)
  local copies, waits for them, and re-layouts  94.3 us (25%)
  blocking collectives  73.7 us (20%)
  matrix products  57.8 us (15%)
  other arithmetic  22.5 us (6%)
  between operations  15.8 us (4%)
  starting transfers between devices  8.35 us (2%)
    psum x1, waiting for transfers between devices, body(): lax.psum((local_kernel, local_bias), ('dp', 'tm', 'space'))  92.7 us
    psum x1, blocking collectives, body(): lax.psum((local_kernel, local_bias), ('dp', 'tm', 'space'))  41.4 us
    dot_general x9, matrix products, body(): jnp.dot(band, taps, preferred_element_type=jnp.float32)  37 us
    reshape x9, local copies, waits for them, and re-layouts, body(): band = padded[kt:kt + frames, ky:ky + rows].reshape(wide_rows, chans)  36.5 us
    dot_general x9, matrix products, body(): lax.dot_general(band, stacked, (((0,), (0,)), ((), ())), preferred_elemen...  20.8 us
    psum x1, blocking collectives, body(): mean = lax.psum(local_sum, ('tm', 'space')) / count  18.5 us
    unnamed x68, local copies, waits for them, and re-layouts  15.4 us
    psum x1, blocking collectives, body(): lax.psum(jnp.sum(spread * spread, axis=(0, 1, 2, 4)), ('tm', 'space'))  13.7 us
  transfers between devices with their start and end apart: 4, of which 2 were waited for; matrix products, arithmetic and copies ran while one was open for 3% of the time, Pallas kernels for 0%

commit v1 on v0

--- a/solution.py
+++ b/solution.py
@@ -80,7 +80,7 @@
     output = ((video[0].astype(jnp.float32) + conv + conv_bias) * mask).astype(jnp.bfloat16)[None]
     local_kernel = jnp.concatenate(grads, axis=0)
     local_bias = jnp.sum(masked.reshape(-1, chans).astype(jnp.float32), axis=0)
-    summed, grad_bias = lax.psum((local_kernel, local_bias), ("dp", "tm", "space"))
+    summed, grad_bias = lax.psum(lax.psum((local_kernel, local_bias), ("tm", "space")), "dp")
     return (output, summed.reshape(3, 3, 3, chans, chans), grad_bias)
 
 

time: 373 us -> 370 us (level)
  blocking collectives: 73.7 us -> 43.1 us
  waiting for transfers between devices: 94.9 us -> 122 us
    psum x1, blocking collectives: 41.4 us -> 10.3 us  [body(): lax.psum(lax.psum((local_kernel, local_bias), ('tm', 'space')), 'dp')]
    psum x1 -> x2, waiting for transfers between devices: 92.7 us -> 120 us  [the longest x1 64.1 us: body(): lax.psum((local_kernel, local_bias), ('tm', 'space'))]
  transfers between devices with their start and end apart: 4 -> 5, of which waited for: 2 -> 3; matrix products, arithmetic and copies ran while one was open for 3% -> 3% of each run, Pallas kernels for 0% -> 0%
where the time goes in v1:
time: 370 us; the launch traced here: 364 us
  waiting for transfers between devices  122 us (33%)
  local copies, waits for them, and re-layouts  94.3 us (25%)
  matrix products  57.8 us (16%)
  blocking collectives  43.1 us (12%)
  other arithmetic  22 us (6%)
  between operations  15.8 us (4%)
  starting transfers between devices  8.4 us (2%)
    psum x1, waiting for transfers between devices, body(): lax.psum((local_kernel, local_bias), ('tm', 'space'))  64.1 us
    psum x1, waiting for transfers between devices, body(): lax.psum(lax.psum((local_kernel, local_bias), ('tm', 'space')), 'dp')  56.1 us
    dot_general x9, matrix products, body(): jnp.dot(band, taps, preferred_element_type=jnp.float32)  37 us
    reshape x9, local copies, waits for them, and re-layouts, body(): band = padded[kt:kt + frames, ky:ky + rows].reshape(wide_rows, chans)  36.6 us
    dot_general x9, matrix products, body(): lax.dot_general(band, stacked, (((0,), (0,)), ((), ())), preferred_elemen...  20.8 us
    psum x1, blocking collectives, body(): mean = lax.psum(local_sum, ('tm', 'space')) / count  18.5 us
    unnamed x68, local copies, waits for them, and re-layouts  15.5 us
    psum x1, blocking collectives, body(): lax.psum(jnp.sum(spread * spread, axis=(0, 1, 2, 4)), ('tm', 'space'))  14.2 us
  transfers between devices with their start and end apart: 5, of which 3 were waited for; matrix products, arithmetic and copies ran while one was open for 3% of the time, Pallas kernels for 0%

profile of v1, /device:TPU:0, one launch (start us, length us, event | category | flops | bytes accessed | tf_op | source)
XLA Modules:
  0.0 364.0 jit_solution(14880789963227678747)
XLA Ops:
  8.0 2.8 fusion.26
  11.0 0.1 reduce_sum.36
  11.1 18.5 %psum.42 = f32[32]{0:T(128)S(1)} all-reduce(f32[32]{0:T(128)S(1)} %reduce_sum.36), channel_id=1, replica_groups=mesh['dp'=4,'tm'=2,'space'=4] {'tm','space'}, use_global_device_ids=true, to_apply=%region_2.0 | all-reduce | flops 32 | bytes 256 | tf_op jit(solution)/shard_map/psum | solution.py:41
  29.7 0.1 sub.20
  29.8 2.8 convert_reduce_fusion
  32.7 0.1 reduce_sum.46
  32.8 14.2 %all-reduce.4 = (f32[32]{0:T(128)S(1)}, f32[128]{0:T(128)}) all-reduce(f32[32]{0:T(128)S(1)} %reduce_sum.46, f32[128]{0:T(128)S(1)} %get-tuple-element.3), channel_id=1, replica_groups=mesh['dp'=4,'tm'=2,'space'=4] {'tm','space'}, use_global_device_ids=true, to_apply=%region_5.6 | all-reduce | flops 160 | bytes 1280 | tf_op jit(solution)/shard_map/psum | solution.py:43
  47.1 0.1 mul.88
  47.2 1.6 fusion.18
  49.0 2.6 collective-permute-start
  51.6 2.2 collective-permute-done
  53.8 0.8 pad_maximum_fusion.1
  54.6 3.9 %collective-permute-start.1 = (bf16[1,6,1,128,128]{4,3,2,1,0:T(8,128)(2,1)}, bf16[1,6,1,128,128]{4,3,2,1,0:T(8,128)(2,1)}, u32[]{:S(2)}, u32[]{:S(2)}) collective-permute-start(bf16[1,6,1,128,128]{4,3,2,1,0:T(8,128)(2,1)} %get-tuple-element.16), channel_id=1, source_target_pairs={{0,1},{1,2},{2,3},{4,5},{5,6},{6,7},{8,9},{9,10},{10,11},{12,13},{... | collective-permute-start | bytes 589832 | tf_op jit(solution)/shard_map/ppermute | solution.py:20
  58.6 1.7 collective-permute-start.2
  60.3 0.8 fusion.46
  61.1 1.6 copy.65
  62.8 1.6 copy.64
  64.4 1.6 copy.63
  66.1 1.6 copy.62
  67.7 1.6 copy.61
  69.3 1.6 copy.60
  71.0 0.8 copy.59
  71.7 0.1 copy.58
  71.9 0.1 copy.57
  72.0 2.0 maximum_bitcast_fusion
  74.0 10.9 %pad_slice_fusion = (bf16[4,16,130,128]{3,2,1,0:T(8,128)(2,1)}, bf16[4,16,130,128]{3,2,1,0:T(8,128)(2,1)}, bf16[4,16,130,128]{3,2,1,0:T(8,128)(2,1)}, bf16[4,16,...) fusion(bf16[6,18,128,128]{3,2,1,0:T(8,128)(2,1)S(1)} %maximum_b, ...), kind=kLoop, calls=%fused_computation.67 | loop fusion | bytes 22708224 | tf_op jit(solution)/shard_map/slice | solution.py:65
  84.9 4.1 %reshape.166 = bf16[8320,128]{1,0:T(8,128)(2,1)} reshape(bf16[4,16,130,128]{3,2,1,0:T(8,128)(2,1)} %get-tuple-element.7) | data formatting | bytes 4259840 | tf_op jit(solution)/shard_map/reshape | solution.py:65
  89.0 4.0 %reshape.152 = bf16[8320,128]{1,0:T(8,128)(2,1)} reshape(bf16[4,16,130,128]{3,2,1,0:T(8,128)(2,1)} %get-tuple-element.8) | data formatting | bytes 4259840 | tf_op jit(solution)/shard_map/reshape | solution.py:65
  93.0 4.1 %reshape.154 = bf16[8320,128]{1,0:T(8,128)(2,1)} reshape(bf16[4,16,130,128]{3,2,1,0:T(8,128)(2,1)} %get-tuple-element.9) | data formatting | bytes 4259840 | tf_op jit(solution)/shard_map/reshape | solution.py:65
  97.1 4.1 %reshape.156 = bf16[8320,128]{1,0:T(8,128)(2,1)} reshape(bf16[4,16,130,128]{3,2,1,0:T(8,128)(2,1)} %get-tuple-element.10) | data formatting | bytes 4259840 | tf_op jit(solution)/shard_map/reshape | solution.py:65
  101.1 4.1 %reshape.158 = bf16[8320,128]{1,0:T(8,128)(2,1)} reshape(bf16[4,16,130,128]{3,2,1,0:T(8,128)(2,1)} %get-tuple-element.11) | data formatting | bytes 4259840 | tf_op jit(solution)/shard_map/reshape | solution.py:65
  105.2 4.1 %reshape.160 = bf16[8320,128]{1,0:T(8,128)(2,1)} reshape(bf16[4,16,130,128]{3,2,1,0:T(8,128)(2,1)} %get-tuple-element.12) | data formatting | bytes 4259840 | tf_op jit(solution)/shard_map/reshape | solution.py:65
  109.3 4.0 %reshape.162 = bf16[8320,128]{1,0:T(8,128)(2,1)} reshape(bf16[4,16,130,128]{3,2,1,0:T(8,128)(2,1)} %get-tuple-element.13) | data formatting | bytes 4259840 | tf_op jit(solution)/shard_map/reshape | solution.py:65
  113.3 4.0 %reshape.164 = bf16[8320,128]{1,0:T(8,128)(2,1)} reshape(bf16[4,16,130,128]{3,2,1,0:T(8,128)(2,1)} %get-tuple-element.14) | data formatting | bytes 4259840 | tf_op jit(solution)/shard_map/reshape | solution.py:65
  117.4 4.2 %reshape.150 = bf16[8320,128]{1,0:T(8,128)(2,1)} reshape(bf16[4,16,130,128]{3,2,1,0:T(8,128)(2,1)} %get-tuple-element.15) | data formatting | bytes 4259840 | tf_op jit(solution)/shard_map/reshape | solution.py:65
  121.5 3.4 fusion.47
  125.0 3.6 convolution_add_fusion.7
  128.6 3.6 convolution_add_fusion.6
  132.2 3.6 convolution_add_fusion.5
  135.8 3.6 convolution_add_fusion.4
  139.4 3.6 convolution_add_fusion.3
  143.1 3.6 convolution_add_fusion.2
  146.7 3.8 %convolution_add_fusion.1 = f32[8320,384]{1,0:T(8,128)S(1)} fusion(f32[8320,384]{1,0:T(8,128)S(1)} %convolution_add_fusion.2, bf16[8320,128]{1,0:T(8,128)(2,1)} %reshape.164, bf16[128,384]{0,1:T(8,128)(2,1)S(1)} %bitcast.176), kind=kOutput, calls=%fused_computation.3 | convolution fusion | flops 821084160 | bytes 27787264 | tf_op jit(solution)/shard_map/dot_general | solution.py:67
  150.5 8.2 %convolution_add_fusion = f32[8320,384]{1,0:T(8,128)} fusion(f32[8320,384]{1,0:T(8,128)S(1)} %convolution_add_fusion.1, bf16[8320,128]{1,0:T(8,128)(2,1)} %reshape.166, bf16[128,384]{0,1:T(8,128)(2,1)S(1)} %bitcast.175), kind=kOutput, calls=%fused_computation.2 | convolution fusion | flops 821084160 | bytes 27787264 | tf_op jit(solution)/shard_map/dot_general | solution.py:67
  158.7 12.0 %reshape.168 = f32[4,16,130,384]{3,2,1,0:T(8,128)} reshape(f32[8320,384]{1,0:T(8,128)} %convolution_add_fusion) | data formatting | bytes 25559040 | tf_op jit(solution)/shard_map/reshape | solution.py:74
  170.7 7.8 %fusion.20 = (bf16[4,16,128,128]{3,2,1,0:T(8,128)(2,1)S(1)}, bf16[1,4,16,128,128]{4,3,2,1,0:T(8,128)(2,1)}) fusion(bf16[1,4,16,128,128]{4,3,2,1,0:T(8,128)(2,1)} %param.13, f32[4]{0:T(128)S(1)} %compare_convert_fusion, f32[128]{0:T(128)S(1)} %copy-done.23, f32[4,16,130,384]{3,2,1,0:T(8,128)} %reshape.168, bf16[1,4,16,128,128]{4,3,2,1,0:T(8,128)(2,1)S(1)} %copy-done.1), kind=kLoop, calls=%fused_computation.37 | loop fusion | flops 10485760 | bytes 20972048 | tf_op jit(solution)/shard_map/convert_element_type | solution.py:51
  178.6 3.9 %fusion.5 = bf16[4,16,130,384]{3,2,1,0:T(8,128)(2,1)} fusion(bf16[4,16,128,128]{3,2,1,0:T(8,128)(2,1)S(1)} %get-tuple-element.27), kind=kLoop, calls=%fused_computation.17 | loop fusion | flops 44728320 | bytes 8486912 | tf_op jit(solution)/shard_map/concatenate | solution.py:52
  182.5 8.5 %reshape.169 = bf16[8320,384]{1,0:T(8,128)(2,1)} reshape(bf16[4,16,130,384]{3,2,1,0:T(8,128)(2,1)} %fusion.5) | data formatting | bytes 12779520 | tf_op jit(solution)/shard_map/reshape | solution.py:59
  191.0 9.4 %copy.29 = bf16[384,8320]{1,0:T(8,128)(2,1)} copy(bf16[384,8320]{0,1:T(8,128)(2,1)} %bitcast.163) | data formatting | bytes 12779520 | tf_op jit(solution)/shard_map/dot_general | solution.py:68
  200.4 4.9 %fusion.27 = f32[128,3,128]{2,0,1:T(8,128)S(1)} fusion(bf16[3,128,8320]{2,1,0:T(8,128)(2,1)} %bitcast.154, bf16[8320,128]{1,0:T(8,128)(2,1)S(1)} %copy-done.5), kind=kOutput, calls=%fused_computation.48 | convolution fusion | flops 817889280 | bytes 8716288 | tf_op jit(solution)/shard_map/dot_general | solution.py:68
  205.4 0.3 copy-done.9
  205.7 2.0 fusion.29
  207.7 2.0 fusion.31
  209.7 2.0 fusion.33
  211.7 2.0 fusion.35
  213.7 2.0 fusion.37
  215.8 2.0 fusion.39
  217.8 2.0 fusion.41
  219.8 2.0 fusion.43
  222.0 1.2 copy-done.12
  223.3 64.1 %all-reduce.8.cloned.1.call-done = f32[3456,128]{1,0:T(8,128)} async-done(((f32[3456,128]{1,0:T(8,128)}), f32[3456,128]{1,0:T(8,128)}) %all-reduce.8.cloned.1.call-update) | async-done | bytes 1769488 | tf_op jit(solution)/shard_map/psum | solution.py:83
  287.4 10.3 %psum.47 = f32[128]{0:T(128)} all-reduce(f32[128]{0:T(128)S(1)} %copy-done.24), channel_id=1, replica_groups=mesh['dp'=4,'tm'=2,'space'=4] {'dp'}, use_global_device_ids=true, to_apply=%region_10.11 | all-reduce | flops 128 | bytes 1024 | tf_op jit(solution)/shard_map/psum | solution.py:83
  297.8 56.1 %all-reduce.10.cloned.1.call-done = f32[3,3,3,128,128]{4,3,2,1,0:T(8,128)} async-done(((f32[3,3,3,128,128]{4,3,2,1,0:T(8,128)}), f32[3,3,3,128,128]{4,3,2,1,0:T(8,128)}) %all-reduce.10.cloned.1.call-update) | async-done | bytes 1769488 | tf_op jit(solution)/shard_map/psum | solution.py:83
  353.9 2.9 copy.77
  (71 shorter events, 0.8 us)
Async XLA Ops:
  7.2 22.6 %copy-start.1 = (bf16[1,4,16,128,128]{4,3,2,1,0:T(8,128)(2,1)S(1)}, bf16[1,4,16,128,128]{4,3,2,1,0:T(8,128)(2,1)}, u32[]{:S(2)}) copy-start(bf16[1,4,16,128,128]{4,3,2,1,0:T(8,128)(2,1)} %param.7) | copy-start | bytes 6291460
  7.2 40.0 %copy-start.21 = (f32[128]{0:T(128)S(1)}, f32[128]{0:T(128)}, u32[]{:S(2)}) copy-start(f32[128]{0:T(128)} %param.10) | copy-start | bytes 1540
  7.2 40.0 %copy-start.22 = (f32[128]{0:T(128)S(1)}, f32[128]{0:T(128)}, u32[]{:S(2)}) copy-start(f32[128]{0:T(128)} %param.9) | copy-start | bytes 1540
  7.2 280.2 %all-reduce.8.cloned.1.call-start = ((), (), s32[]{:S(2)}) async-start(), calls=%async_computation | async-start | bytes 3538944 | tf_op jit(solution)/shard_map/psum | solution.py:83
  48.9 12.3 %copy-start.10 = (bf16[1,4,16,128,128]{4,3,2,1,0:T(8,128)(2,1)}, bf16[1,4,16,128,128]{4,3,2,1,0:T(8,128)(2,1)S(1)}, u32[]{:S(2)}) copy-start(bf16[1,4,16,128,128]{4,3,2,1,0:T(8,128)(2,1)S(1)} %fusion.18) | copy-start | bytes 6291460
  48.9 11.4 %copy-start.13 = (bf16[3,3,3,128,128]{4,3,2,1,0:T(8,128)(2,1)S(1)}, bf16[3,3,3,128,128]{4,3,2,1,0:T(8,128)(2,1)}, u32[]{:S(2)}) copy-start(bf16[3,3,3,128,128]{4,3,2,1,0:T(8,128)(2,1)} %param.11) | copy-start | bytes 2654212
  49.0 4.8 %collective-permute-start = (bf16[1,2,16,128,128]{4,3,2,1,0:T(8,128)(2,1)S(1)}, bf16[1,2,16,128,128]{4,3,2,1,0:T(8,128)(2,1)S(1)}, u32[]{:S(2)}, u32[]{:S(2)}) collective-permute-start(bf16[1,2,16,128,128]{4,3,2,1,0:T(8,128)(2,1)S(1)} %slice.96), channel_id=1, source_target_pairs={{0,4},{1,5},{2,6},{3,7},{8,12},{9,13},{10,14},{11,15},{16,20},{17,... | collective-permute-start | bytes 3145736 | tf_op jit(solution)/shard_map/ppermute | solution.py:12
  54.6 17.4 %collective-permute-start.1 = (bf16[1,6,1,128,128]{4,3,2,1,0:T(8,128)(2,1)}, bf16[1,6,1,128,128]{4,3,2,1,0:T(8,128)(2,1)}, u32[]{:S(2)}, u32[]{:S(2)}) collective-permute-start(bf16[1,6,1,128,128]{4,3,2,1,0:T(8,128)(2,1)} %get-tuple-element.16), channel_id=1, source_target_pairs={{0,1},{1,2},{2,3},{4,5},{5,6},{6,7},{8,9},{9,10},{10,11},{12,13},{... | collective-permute-start | bytes 589832 | tf_op jit(solution)/shard_map/ppermute | solution.py:20
  58.6 13.5 %collective-permute-start.2 = (bf16[1,6,1,128,128]{4,3,2,1,0:T(8,128)(2,1)}, bf16[1,6,1,128,128]{4,3,2,1,0:T(8,128)(2,1)}, u32[]{:S(2)}, u32[]{:S(2)}) collective-permute-start(bf16[1,6,1,128,128]{4,3,2,1,0:T(8,128)(2,1)} %get-tuple-element.17), channel_id=1, source_target_pairs={{1,0},{2,1},{3,2},{5,4},{6,5},{7,6},{9,8},{10,9},{11,10},{13,12},{... | collective-permute-start | bytes 589832 | tf_op jit(solution)/shard_map/ppermute | solution.py:23
  125.0 3.6 copy-start.20
  128.6 3.6 copy-start.19
  132.2 3.6 copy-start.18
  135.8 3.6 copy-start.17
  139.4 3.6 copy-start.16
  143.1 3.6 copy-start.15
  146.7 3.8 %copy-start.14 = (bf16[1,1,3,128,128]{3,4,2,1,0:T(8,128)(2,1)S(1)}, bf16[1,1,3,128,128]{3,4,2,1,0:T(8,128)(2,1)}, u32[]{:S(2)}) copy-start(bf16[1,1,3,128,128]{3,4,2,1,0:T(8,128)(2,1)} %copy.65) | copy-start | bytes 294916
  158.7 12.0 %copy-start.23 = (f32[128]{0:T(128)S(1)}, f32[128]{0:T(128)}, u32[]{:S(2)}) copy-start(f32[128]{0:T(128)} %param.12) | copy-start | bytes 1540
  191.0 9.4 %copy-start.5 = (bf16[8320,128]{1,0:T(8,128)(2,1)S(1)}, bf16[8320,128]{1,0:T(8,128)(2,1)}, u32[]{:S(2)}) copy-start(bf16[8320,128]{1,0:T(8,128)(2,1)} %reshape.166) | copy-start | bytes 6389764
  200.4 5.0 %copy-start = (bf16[384,8320]{1,0:T(8,128)(2,1)S(1)}, bf16[384,8320]{1,0:T(8,128)(2,1)}, u32[]{:S(2)}) copy-start(bf16[384,8320]{1,0:T(8,128)(2,1)} %copy.29) | copy-start | bytes 19169284
  200.4 5.3 %copy-start.9 = (bf16[8320,128]{1,0:T(8,128)(2,1)S(1)}, bf16[8320,128]{1,0:T(8,128)(2,1)}, u32[]{:S(2)}) copy-start(bf16[8320,128]{1,0:T(8,128)(2,1)} %reshape.164) | copy-start | bytes 6389764
  205.7 2.0 copy-start.8
  207.7 2.0 copy-start.7
  209.7 2.0 copy-start.6
  211.7 2.0 copy-start.4
  213.7 2.0 copy-start.3
  215.8 2.0 copy-start.2
  217.8 2.0 copy-start.11
  221.8 65.7 %copy-start.24 = (f32[128]{0:T(128)S(1)}, f32[128]{0:T(128)}, u32[]{:S(2)}) copy-start(f32[128]{0:T(128)} %get-tuple-element.6) | copy-start | bytes 1540
  222.0 1.2 copy-start.12
  223.2 130.6 %all-reduce.10.cloned.1.call-start = ((), (), s32[]{:S(2)}) async-start(), calls=%async_computation.1 | async-start | bytes 3538944 | tf_op jit(solution)/shard_map/psum | solution.py:83
Sparse Core Ops, SparseCore 0:
  223.3 64.0 all-reduce.7
  290.6 63.2 all-reduce.9
